TPU v7x, 512 devices: a whole 4x4x16 slice. The times are simulated.
512 devices in a mesh: ctx: 16 (over y, z_lo), exp: 32 (over z_hi, x, core).
Axes of the slice: x: 4, y: 4, z: 16 (z_hi: 4, z_lo: 4; z = z_hi * 4 + z_lo), core: 2. Of those that a mesh axis runs over, the one named last changes fastest.
Arguments:
- query: bfloat16 [32, 1024, 2048], P('exp', 'ctx'), may hold values from -24 to 24
- key_value: bfloat16 [32, 1024, 2, 256], P('exp', 'ctx'), may hold values from -24 to 24
- positions: int32 [32, 1024], P('exp', 'ctx'), may hold values from 0 to 1023, as said below
- resid: bfloat16 [32, 1024, 1440], P('exp', 'ctx'), may hold values from -6 to 6
- sinks: float32 [32], replicated, may hold values from -2 to 3
- o_weight: bfloat16 [2048, 1440], P('exp'), may hold values from -0.125 to 0.125
- norm_gain: float32 [1440], replicated, may hold values from 0.25 to 1.75
- expert_ids: int32 [32, 1024, 4], P('exp', 'ctx'), may hold values from 0 to 127, all different within a row; in each aligned block of 64 rows (0 to 63, 64 to 127, ..., all dimensions but the last counted through in order) at most 2 rows name the same one
- route_weights: float32 [32, 1024, 4], P('exp', 'ctx'), may hold values from 0.1 to 0.5
- w_gate: bfloat16 [1440, 184320], P(None, ('ctx', 'exp')), may hold values from -0.15625 to 0.15625
- w_up: bfloat16 [1440, 184320], P(None, ('ctx', 'exp')), may hold values from -0.15625 to 0.15625
- w_down: bfloat16 [184320, 1440], P(('ctx', 'exp')), may hold values from -0.15625 to 0.15625
Outputs:
- out: bfloat16 [32, 1024, 1440], P('exp', 'ctx')
Inputs may be any that keep to these rules, and one draw needn't show every extreme that they name: Within each sequence every position appears once; the 64 stored rows of one device are two runs of 32 consecutive ascending positions, each run starting at a multiple of 32. `expert_ids`: each row names 4 different experts; among the 64 rows of one device no expert is named more than 2 times, a bound that some block reaches.
All inputs are finite; a program needn't handle non-finite values.
Results may differ from a plain program's by a relative error of at most 0.0075.
Values may be sent and summed in bfloat16 or wider, within the bound.
No kernel may reach another device: no remote copies, remote signals or barrier semaphores. Data moves between devices by JAX's collectives and lax.ppermute only.
A program may use at most 64 MiB of HBM per device.

v0:
```python
import math
import jax
import jax.numpy as jnp
from jax import lax
from jax.sharding import PartitionSpec as P

D = 1440
QH = 32
KVH = 4
HD = 64
TOP = 4
SLICES = 4
NEG_FILL = -1e30


def passed_along(value, axis, by):
    length = lax.axis_size(axis)
    return lax.ppermute(value, axis, [(i, (i + by) % length) for i in range(length)])


def attend_block(grouped, keys, values, query_pos, key_pos, state):
    run_max, run_sum, accum = state
    scores = jnp.einsum("rgjd,sgd->gjrs", grouped, keys, preferred_element_type=jnp.float32) * (
        1.0 / math.sqrt(HD)
    )
    allowed = key_pos[None, :] <= query_pos[:, None]
    scores = jnp.where(allowed[None, None], scores, NEG_FILL)
    new_max = jnp.maximum(run_max, jnp.max(scores, axis=-1))
    factor = jnp.exp(run_max - new_max)
    weights = jnp.exp(scores - new_max[..., None])
    run_sum = run_sum * factor + jnp.sum(weights, axis=-1)
    accum = accum * factor[..., None] + jnp.einsum(
        "gjrs,sgd->gjrd", weights, values.astype(jnp.float32), precision=lax.Precision.HIGHEST
    )
    return (new_max, run_sum, accum)


def body(
    query,
    key_value,
    positions,
    resid,
    sinks,
    o_weight,
    norm_gain,
    expert_ids,
    route_weights,
    w_gate,
    w_up,
    w_down,
):
    rows = query.shape[1]
    group = QH // KVH
    grouped = query[0].reshape(rows, KVH, group, HD)
    own_kv = key_value[0]
    own_pos = positions[0]
    start_max = jnp.broadcast_to(sinks.reshape(KVH, group)[:, :, None], (KVH, group, rows))
    state = (
        start_max,
        jnp.ones((KVH, group, rows), jnp.float32),
        jnp.zeros((KVH, group, rows, HD), jnp.float32),
    )

    def take(block, block_pos, carry):
        width = block.shape[0]
        keys = block[:, 0].reshape(width, KVH, HD)
        values = block[:, 1].reshape(width, KVH, HD)
        return attend_block(grouped, keys, values, own_pos, block_pos, carry)

    state = take(own_kv, own_pos, state)

    def turn(step, carry):
        block, block_pos, inner = carry
        block, block_pos = passed_along((block, block_pos), "ctx", 1)
        return (block, block_pos, take(block, block_pos, inner))

    state = lax.fori_loop(0, lax.axis_size("ctx") - 1, turn, (own_kv, own_pos, state))[2]
    run_max, run_sum, accum = state
    attended = accum / run_sum[..., None]
    attended = jnp.transpose(attended, (2, 0, 1, 3)).reshape(rows, QH * HD).astype(jnp.bfloat16)
    projected = jnp.dot(
        attended,
        lax.all_gather(o_weight, "exp", axis=0, tiled=True),
        preferred_element_type=jnp.float32,
    )
    mixed = resid[0].astype(jnp.float32) + projected
    normed = (
        mixed * lax.rsqrt(jnp.mean(mixed * mixed, axis=-1, keepdims=True) + 1e-05) * norm_gain
    ).astype(jnp.bfloat16)
    n_ctx = lax.axis_size("ctx")
    n_exp = lax.axis_size("exp")
    n_experts = n_ctx * n_exp // SLICES
    per_row = n_exp // SLICES
    cap = max(2, rows * TOP // n_experts)
    n_slots = n_experts * cap
    chosen = expert_ids[0].reshape(rows * TOP)
    onehot = (chosen[:, None] == jnp.arange(n_experts, dtype=jnp.int32)[None, :]).astype(jnp.int32)
    rank = jnp.sum((jnp.cumsum(onehot, axis=0) - onehot) * onehot, axis=1)
    slot = (chosen % per_row * n_ctx + chosen // per_row) * cap + rank
    source = (
        jnp.zeros((n_slots,), jnp.int32)
        .at[slot]
        .set(jnp.arange(rows * TOP, dtype=jnp.int32) // TOP)
    )
    filled = jnp.zeros((n_slots,), jnp.bool_).at[slot].set(True)
    outgoing = jnp.where(filled[:, None], normed[source], jnp.zeros((), jnp.bfloat16)).reshape(
        per_row, n_ctx, cap, D
    )
    arrived = lax.all_to_all(outgoing, "ctx", split_axis=1, concat_axis=1, tiled=True)
    copies = jnp.repeat(arrived, SLICES, axis=0)
    block = lax.all_to_all(copies, "exp", split_axis=0, concat_axis=0, tiled=True)
    flat = block.reshape(-1, D)
    gate = jnp.dot(flat, w_gate, preferred_element_type=jnp.float32)
    lifted = jnp.dot(flat, w_up, preferred_element_type=jnp.float32)
    active = (gate * jax.nn.sigmoid(1.702 * gate) * (lifted + 1.0)).astype(jnp.bfloat16)
    back = lax.all_to_all(
        jnp.dot(active, w_down, preferred_element_type=jnp.float32)
        .astype(jnp.bfloat16)
        .reshape(block.shape),
        "exp",
        split_axis=0,
        concat_axis=0,
        tiled=True,
    )
    count = back.shape[1]
    summed = jnp.sum(back.reshape(per_row, SLICES, count, cap, D).astype(jnp.float32), axis=1)
    result = summed.astype(jnp.bfloat16)
    returned = lax.all_to_all(result, "ctx", split_axis=1, concat_axis=1, tiled=True)
    picked = returned.reshape(n_slots, D)[slot].astype(jnp.float32).reshape(rows, TOP, D)
    final = mixed + jnp.sum(route_weights[0][:, :, None] * picked, axis=1)
    return final.astype(jnp.bfloat16)[None]


def solution(mesh):
    return jax.shard_map(
        body,
        mesh=mesh,
        in_specs=(
            P("exp", "ctx", None),
            P("exp", "ctx", None, None),
            P("exp", "ctx"),
            P("exp", "ctx", None),
            P(),
            P("exp", None),
            P(),
            P("exp", "ctx", None),
            P("exp", "ctx", None),
            P(None, ("ctx", "exp")),
            P(None, ("ctx", "exp")),
            P(("ctx", "exp"), None),
        ),
        out_specs=P("exp", "ctx", None),
        check_vma=False,
    )
```

profile of v0, /device:TPU:1, one launch (start us, length us, event | category | flops | bytes accessed | tf_op | source)
XLA Modules:
  0.0 688.6 jit_solution(17631098706521870149)
XLA Ops:
  17.1 230.6 %while.18 = (s32[]{:T(128)}, bf16[64,2,256]{2,0,1:T(8,128)(2,1)S(1)}, s32[64]{0:T(128)S(1)}, f32[4,8,64]{2,1,0:T(8,128)S(1)}, f32[4,8,64]{2,1,0:T(8,128)S(1)}, /...) while((s32[]{:T(128)}, ...), condition=%wide.region_5.6_spmd, body=%wide.region_2.5_spmd.sunk | while | flops 118759424 | bytes 3754157 | solution.py:77
  17.1 4.4 collective-permute-start.1
  21.5 3.5 collective-permute-start
  36.8 4.8 collective-permute-done.1
  41.6 4.9 collective-permute-done
  53.0 4.8 collective-permute-done.1
  67.7 4.4 collective-permute-done.1
  81.1 6.7 collective-permute-done.1
  87.9 21.1 %collective-permute-done = bf16[64,2,256]{2,0,1:T(8,128)(2,1)S(1)} collective-permute-done((bf16[64,2,256]{2,0,1:T(8,128)(2,1)S(1)}, bf16[64,2,256]{2,0,1:T(8,128)(2,1)S(1)}, u32[]{:S(2)}, u32[]{:S(2)}) %collective-permute-start) | collective-permute-done | bytes 65568 | tf_op jit(solution)/shard_map/while/body/eval_jaxpr/ppermute | solution.py:18
  115.4 4.8 collective-permute-done.1
  120.2 4.0 collective-permute-done
  130.7 4.4 collective-permute-done.1
  144.1 4.4 collective-permute-done.1
  157.5 4.4 collective-permute-done.1
  170.8 4.4 collective-permute-done.1
  184.2 4.7 collective-permute-done.1
  197.6 4.4 collective-permute-done.1
  211.0 4.4 collective-permute-done.1
  224.8 4.4 collective-permute-done.1
  238.2 4.4 collective-permute-done.1
  252.9 4.1 multiply_reduce_fusion.1
  260.2 16.6 %all_to_all.20 = bf16[8,16,2,1440]{3,2,0,1:T(2,128)(2,1)S(1)} all-to-all(bf16[8,16,2,1440]{3,2,0,1:T(2,128)(2,1)S(1)} %copy.69), channel_id=1, replica_groups=mesh['ctx'=16,'exp'=32] {'ctx'}, dimensions={1} | all-to-all | bytes 1474560 | tf_op jit(solution)/shard_map/all_to_all | solution.py:109
  280.1 183.5 %all_to_all.21 = bf16[32,16,2,1440]{3,2,1,0:T(2,128)(2,1)} all-to-all(bf16[32,16,2,1440]{3,2,1,0:T(2,128)(2,1)S(1)} %bitcast.67), channel_id=1, replica_groups=mesh['ctx'=16,'exp'=32] {'exp'}, dimensions={0} | all-to-all | bytes 5898240 | tf_op jit(solution)/shard_map/all_to_all | solution.py:111
  463.6 7.6 %reshape.250 = bf16[1024,1440]{1,0:T(8,128)(2,1)} reshape(bf16[32,16,2,1440]{3,2,1,0:T(2,128)(2,1)} %all_to_all.21) | data formatting | bytes 5898240 | tf_op jit(solution)/shard_map/reshape | solution.py:112
  471.2 4.4 fusion.37
  475.6 7.4 %convolution_convert_fusion = bf16[1024,1440]{0,1:T(8,128)(2,1)} fusion(bf16[360,1440]{1,0:T(8,128)(2,1)S(1)} %copy-done, f32[1024,360]{0,1:T(8,128)} %fusion.37, bf16[1024,1440]{1,0:T(8,128)(2,1)} %reshape.250, bf16[1440,360]{1,0:T(8,128)(2,1)} %param.24), kind=kOutput, calls=%fused_computation.19 | convolution fusion | flops 2127790080 | bytes 9446400 | tf_op jit(solution)/shard_map/dot_general | solution.py:117
  482.9 4.6 copy.71
  487.5 7.3 %reshape.251 = bf16[32,16,2,1440]{3,2,1,0:T(2,128)(2,1)} reshape(bf16[1024,1440]{1,0:T(8,128)(2,1)} %copy.71) | data formatting | bytes 5898240 | tf_op jit(solution)/shard_map/reshape | solution.py:119
  494.9 149.7 %all_to_all.22 = bf16[32,16,2,1440]{3,2,1,0:T(2,128)(2,1)S(1)} all-to-all(bf16[32,16,2,1440]{3,2,1,0:T(2,128)(2,1)} %reshape.251), channel_id=1, replica_groups=mesh['ctx'=16,'exp'=32] {'exp'}, dimensions={0} | all-to-all | bytes 5898240 | tf_op jit(solution)/shard_map/all_to_all | solution.py:116
  644.5 3.5 bitcast_reduce_fusion
  649.7 3.9 all-to-all-start.3
  653.7 21.3 %all-to-all-done.3 = bf16[8,16,2,1440]{3,2,0,1:T(2,128)(2,1)S(1)} async-done(((bf16[8,16,2,1440]{3,2,0,1:T(2,128)(2,1)}), bf16[8,16,2,1440]{3,2,0,1:T(2,128)(2,1)S(1)}, u32[]{:S(2)}, u32[]{:S(2)}) %all-to-all-start.3) | async-done | bytes 737312 | tf_op jit(solution)/shard_map/all_to_all | solution.py:128
  (295 shorter events, 156.7 us)
Async XLA Ops:
  6.5 246.3 %all-gather.2.cloned.1.call-start = ((), (), s32[]{:S(2)}) async-start(), calls=%async_computation.4 | async-start | bytes 6488064 | tf_op jit(solution)/shard_map/all_gather | solution.py:83
  17.1 10.5 %collective-permute-start.1 = (s32[64]{0:T(128)S(1)}, s32[64]{0:T(128)S(1)}, u32[]{:S(2)}, u32[]{:S(2)}) collective-permute-start(s32[64]{0:T(128)S(1)} %get-tuple-element.176), channel_id=1, source_target_pairs={{0,32},{32,64},{64,96},{96,128},{128,160},{160,192},{192,224},{224... | collective-permute-start | bytes 776 | tf_op jit(solution)/shard_map/while/body/eval_jaxpr/ppermute | solution.py:18
  21.5 8.9 %collective-permute-start = (bf16[64,2,256]{2,0,1:T(8,128)(2,1)S(1)}, bf16[64,2,256]{2,0,1:T(8,128)(2,1)S(1)}, u32[]{:S(2)}, u32[]{:S(2)}) collective-permute-start(bf16[64,2,256]{2,0,1:T(8,128)(2,1)S(1)} %get-tuple-element.175), channel_id=1, source_target_pairs={{0,32},{32,64},{64,96},{96,128},{128,160},{160,192},{192,224},{224... | collective-permute-start | bytes 196616 | tf_op jit(solution)/shard_map/while/body/eval_jaxpr/ppermute | solution.py:18
  32.9 8.6 %collective-permute-start.1 = (s32[64]{0:T(128)S(1)}, s32[64]{0:T(128)S(1)}, u32[]{:S(2)}, u32[]{:S(2)}) collective-permute-start(s32[64]{0:T(128)S(1)} %get-tuple-element.176), channel_id=1, source_target_pairs={{0,32},{32,64},{64,96},{96,128},{128,160},{160,192},{192,224},{224... | collective-permute-start | bytes 776 | tf_op jit(solution)/shard_map/while/body/eval_jaxpr/ppermute | solution.py:18
  34.8 11.7 %collective-permute-start = (bf16[64,2,256]{2,0,1:T(8,128)(2,1)S(1)}, bf16[64,2,256]{2,0,1:T(8,128)(2,1)S(1)}, u32[]{:S(2)}, u32[]{:S(2)}) collective-permute-start(bf16[64,2,256]{2,0,1:T(8,128)(2,1)S(1)} %get-tuple-element.175), channel_id=1, source_target_pairs={{0,32},{32,64},{64,96},{96,128},{128,160},{160,192},{192,224},{224... | collective-permute-start | bytes 196616 | tf_op jit(solution)/shard_map/while/body/eval_jaxpr/ppermute | solution.py:18
  49.1 8.6 %collective-permute-start.1 = (s32[64]{0:T(128)S(1)}, s32[64]{0:T(128)S(1)}, u32[]{:S(2)}, u32[]{:S(2)}) collective-permute-start(s32[64]{0:T(128)S(1)} %get-tuple-element.176), channel_id=1, source_target_pairs={{0,32},{32,64},{64,96},{96,128},{128,160},{160,192},{192,224},{224... | collective-permute-start | bytes 776 | tf_op jit(solution)/shard_map/while/body/eval_jaxpr/ppermute | solution.py:18
  51.0 10.3 %collective-permute-start = (bf16[64,2,256]{2,0,1:T(8,128)(2,1)S(1)}, bf16[64,2,256]{2,0,1:T(8,128)(2,1)S(1)}, u32[]{:S(2)}, u32[]{:S(2)}) collective-permute-start(bf16[64,2,256]{2,0,1:T(8,128)(2,1)S(1)} %get-tuple-element.175), channel_id=1, source_target_pairs={{0,32},{32,64},{64,96},{96,128},{128,160},{160,192},{192,224},{224... | collective-permute-start | bytes 196616 | tf_op jit(solution)/shard_map/while/body/eval_jaxpr/ppermute | solution.py:18
  63.8 8.2 %collective-permute-start.1 = (s32[64]{0:T(128)S(1)}, s32[64]{0:T(128)S(1)}, u32[]{:S(2)}, u32[]{:S(2)}) collective-permute-start(s32[64]{0:T(128)S(1)} %get-tuple-element.176), channel_id=1, source_target_pairs={{0,32},{32,64},{64,96},{96,128},{128,160},{160,192},{192,224},{224... | collective-permute-start | bytes 776 | tf_op jit(solution)/shard_map/while/body/eval_jaxpr/ppermute | solution.py:18
  65.8 8.9 %collective-permute-start = (bf16[64,2,256]{2,0,1:T(8,128)(2,1)S(1)}, bf16[64,2,256]{2,0,1:T(8,128)(2,1)S(1)}, u32[]{:S(2)}, u32[]{:S(2)}) collective-permute-start(bf16[64,2,256]{2,0,1:T(8,128)(2,1)S(1)} %get-tuple-element.175), channel_id=1, source_target_pairs={{0,32},{32,64},{64,96},{96,128},{128,160},{160,192},{192,224},{224... | collective-permute-start | bytes 196616 | tf_op jit(solution)/shard_map/while/body/eval_jaxpr/ppermute | solution.py:18
  77.2 10.6 %collective-permute-start.1 = (s32[64]{0:T(128)S(1)}, s32[64]{0:T(128)S(1)}, u32[]{:S(2)}, u32[]{:S(2)}) collective-permute-start(s32[64]{0:T(128)S(1)} %get-tuple-element.176), channel_id=1, source_target_pairs={{0,32},{32,64},{64,96},{96,128},{128,160},{160,192},{192,224},{224... | collective-permute-start | bytes 776 | tf_op jit(solution)/shard_map/while/body/eval_jaxpr/ppermute | solution.py:18
  79.2 29.8 %collective-permute-start = (bf16[64,2,256]{2,0,1:T(8,128)(2,1)S(1)}, bf16[64,2,256]{2,0,1:T(8,128)(2,1)S(1)}, u32[]{:S(2)}, u32[]{:S(2)}) collective-permute-start(bf16[64,2,256]{2,0,1:T(8,128)(2,1)S(1)} %get-tuple-element.175), channel_id=1, source_target_pairs={{0,32},{32,64},{64,96},{96,128},{128,160},{160,192},{192,224},{224... | collective-permute-start | bytes 196616 | tf_op jit(solution)/shard_map/while/body/eval_jaxpr/ppermute | solution.py:18
  111.5 8.6 %collective-permute-start.1 = (s32[64]{0:T(128)S(1)}, s32[64]{0:T(128)S(1)}, u32[]{:S(2)}, u32[]{:S(2)}) collective-permute-start(s32[64]{0:T(128)S(1)} %get-tuple-element.176), channel_id=1, source_target_pairs={{0,32},{32,64},{64,96},{96,128},{128,160},{160,192},{192,224},{224... | collective-permute-start | bytes 776 | tf_op jit(solution)/shard_map/while/body/eval_jaxpr/ppermute | solution.py:18
  113.5 10.8 %collective-permute-start = (bf16[64,2,256]{2,0,1:T(8,128)(2,1)S(1)}, bf16[64,2,256]{2,0,1:T(8,128)(2,1)S(1)}, u32[]{:S(2)}, u32[]{:S(2)}) collective-permute-start(bf16[64,2,256]{2,0,1:T(8,128)(2,1)S(1)} %get-tuple-element.175), channel_id=1, source_target_pairs={{0,32},{32,64},{64,96},{96,128},{128,160},{160,192},{192,224},{224... | collective-permute-start | bytes 196616 | tf_op jit(solution)/shard_map/while/body/eval_jaxpr/ppermute | solution.py:18
  126.8 8.2 %collective-permute-start.1 = (s32[64]{0:T(128)S(1)}, s32[64]{0:T(128)S(1)}, u32[]{:S(2)}, u32[]{:S(2)}) collective-permute-start(s32[64]{0:T(128)S(1)} %get-tuple-element.176), channel_id=1, source_target_pairs={{0,32},{32,64},{64,96},{96,128},{128,160},{160,192},{192,224},{224... | collective-permute-start | bytes 776 | tf_op jit(solution)/shard_map/while/body/eval_jaxpr/ppermute | solution.py:18
  128.7 8.9 %collective-permute-start = (bf16[64,2,256]{2,0,1:T(8,128)(2,1)S(1)}, bf16[64,2,256]{2,0,1:T(8,128)(2,1)S(1)}, u32[]{:S(2)}, u32[]{:S(2)}) collective-permute-start(bf16[64,2,256]{2,0,1:T(8,128)(2,1)S(1)} %get-tuple-element.175), channel_id=1, source_target_pairs={{0,32},{32,64},{64,96},{96,128},{128,160},{160,192},{192,224},{224... | collective-permute-start | bytes 196616 | tf_op jit(solution)/shard_map/while/body/eval_jaxpr/ppermute | solution.py:18
  140.2 8.2 %collective-permute-start.1 = (s32[64]{0:T(128)S(1)}, s32[64]{0:T(128)S(1)}, u32[]{:S(2)}, u32[]{:S(2)}) collective-permute-start(s32[64]{0:T(128)S(1)} %get-tuple-element.176), channel_id=1, source_target_pairs={{0,32},{32,64},{64,96},{96,128},{128,160},{160,192},{192,224},{224... | collective-permute-start | bytes 776 | tf_op jit(solution)/shard_map/while/body/eval_jaxpr/ppermute | solution.py:18
  142.1 8.9 %collective-permute-start = (bf16[64,2,256]{2,0,1:T(8,128)(2,1)S(1)}, bf16[64,2,256]{2,0,1:T(8,128)(2,1)S(1)}, u32[]{:S(2)}, u32[]{:S(2)}) collective-permute-start(bf16[64,2,256]{2,0,1:T(8,128)(2,1)S(1)} %get-tuple-element.175), channel_id=1, source_target_pairs={{0,32},{32,64},{64,96},{96,128},{128,160},{160,192},{192,224},{224... | collective-permute-start | bytes 196616 | tf_op jit(solution)/shard_map/while/body/eval_jaxpr/ppermute | solution.py:18
  153.6 8.2 %collective-permute-start.1 = (s32[64]{0:T(128)S(1)}, s32[64]{0:T(128)S(1)}, u32[]{:S(2)}, u32[]{:S(2)}) collective-permute-start(s32[64]{0:T(128)S(1)} %get-tuple-element.176), channel_id=1, source_target_pairs={{0,32},{32,64},{64,96},{96,128},{128,160},{160,192},{192,224},{224... | collective-permute-start | bytes 776 | tf_op jit(solution)/shard_map/while/body/eval_jaxpr/ppermute | solution.py:18
  155.5 8.9 %collective-permute-start = (bf16[64,2,256]{2,0,1:T(8,128)(2,1)S(1)}, bf16[64,2,256]{2,0,1:T(8,128)(2,1)S(1)}, u32[]{:S(2)}, u32[]{:S(2)}) collective-permute-start(bf16[64,2,256]{2,0,1:T(8,128)(2,1)S(1)} %get-tuple-element.175), channel_id=1, source_target_pairs={{0,32},{32,64},{64,96},{96,128},{128,160},{160,192},{192,224},{224... | collective-permute-start | bytes 196616 | tf_op jit(solution)/shard_map/while/body/eval_jaxpr/ppermute | solution.py:18
  167.0 8.2 %collective-permute-start.1 = (s32[64]{0:T(128)S(1)}, s32[64]{0:T(128)S(1)}, u32[]{:S(2)}, u32[]{:S(2)}) collective-permute-start(s32[64]{0:T(128)S(1)} %get-tuple-element.176), channel_id=1, source_target_pairs={{0,32},{32,64},{64,96},{96,128},{128,160},{160,192},{192,224},{224... | collective-permute-start | bytes 776 | tf_op jit(solution)/shard_map/while/body/eval_jaxpr/ppermute | solution.py:18
  168.9 8.9 %collective-permute-start = (bf16[64,2,256]{2,0,1:T(8,128)(2,1)S(1)}, bf16[64,2,256]{2,0,1:T(8,128)(2,1)S(1)}, u32[]{:S(2)}, u32[]{:S(2)}) collective-permute-start(bf16[64,2,256]{2,0,1:T(8,128)(2,1)S(1)} %get-tuple-element.175), channel_id=1, source_target_pairs={{0,32},{32,64},{64,96},{96,128},{128,160},{160,192},{192,224},{224... | collective-permute-start | bytes 196616 | tf_op jit(solution)/shard_map/while/body/eval_jaxpr/ppermute | solution.py:18
  180.4 8.5 %collective-permute-start.1 = (s32[64]{0:T(128)S(1)}, s32[64]{0:T(128)S(1)}, u32[]{:S(2)}, u32[]{:S(2)}) collective-permute-start(s32[64]{0:T(128)S(1)} %get-tuple-element.176), channel_id=1, source_target_pairs={{0,32},{32,64},{64,96},{96,128},{128,160},{160,192},{192,224},{224... | collective-permute-start | bytes 776 | tf_op jit(solution)/shard_map/while/body/eval_jaxpr/ppermute | solution.py:18
  182.3 8.9 %collective-permute-start = (bf16[64,2,256]{2,0,1:T(8,128)(2,1)S(1)}, bf16[64,2,256]{2,0,1:T(8,128)(2,1)S(1)}, u32[]{:S(2)}, u32[]{:S(2)}) collective-permute-start(bf16[64,2,256]{2,0,1:T(8,128)(2,1)S(1)} %get-tuple-element.175), channel_id=1, source_target_pairs={{0,32},{32,64},{64,96},{96,128},{128,160},{160,192},{192,224},{224... | collective-permute-start | bytes 196616 | tf_op jit(solution)/shard_map/while/body/eval_jaxpr/ppermute | solution.py:18
  193.8 8.2 %collective-permute-start.1 = (s32[64]{0:T(128)S(1)}, s32[64]{0:T(128)S(1)}, u32[]{:S(2)}, u32[]{:S(2)}) collective-permute-start(s32[64]{0:T(128)S(1)} %get-tuple-element.176), channel_id=1, source_target_pairs={{0,32},{32,64},{64,96},{96,128},{128,160},{160,192},{192,224},{224... | collective-permute-start | bytes 776 | tf_op jit(solution)/shard_map/while/body/eval_jaxpr/ppermute | solution.py:18
  195.7 8.9 %collective-permute-start = (bf16[64,2,256]{2,0,1:T(8,128)(2,1)S(1)}, bf16[64,2,256]{2,0,1:T(8,128)(2,1)S(1)}, u32[]{:S(2)}, u32[]{:S(2)}) collective-permute-start(bf16[64,2,256]{2,0,1:T(8,128)(2,1)S(1)} %get-tuple-element.175), channel_id=1, source_target_pairs={{0,32},{32,64},{64,96},{96,128},{128,160},{160,192},{192,224},{224... | collective-permute-start | bytes 196616 | tf_op jit(solution)/shard_map/while/body/eval_jaxpr/ppermute | solution.py:18
  207.2 8.2 %collective-permute-start.1 = (s32[64]{0:T(128)S(1)}, s32[64]{0:T(128)S(1)}, u32[]{:S(2)}, u32[]{:S(2)}) collective-permute-start(s32[64]{0:T(128)S(1)} %get-tuple-element.176), channel_id=1, source_target_pairs={{0,32},{32,64},{64,96},{96,128},{128,160},{160,192},{192,224},{224... | collective-permute-start | bytes 776 | tf_op jit(solution)/shard_map/while/body/eval_jaxpr/ppermute | solution.py:18
  209.1 9.3 %collective-permute-start = (bf16[64,2,256]{2,0,1:T(8,128)(2,1)S(1)}, bf16[64,2,256]{2,0,1:T(8,128)(2,1)S(1)}, u32[]{:S(2)}, u32[]{:S(2)}) collective-permute-start(bf16[64,2,256]{2,0,1:T(8,128)(2,1)S(1)} %get-tuple-element.175), channel_id=1, source_target_pairs={{0,32},{32,64},{64,96},{96,128},{128,160},{160,192},{192,224},{224... | collective-permute-start | bytes 196616 | tf_op jit(solution)/shard_map/while/body/eval_jaxpr/ppermute | solution.py:18
  220.9 8.2 %collective-permute-start.1 = (s32[64]{0:T(128)S(1)}, s32[64]{0:T(128)S(1)}, u32[]{:S(2)}, u32[]{:S(2)}) collective-permute-start(s32[64]{0:T(128)S(1)} %get-tuple-element.176), channel_id=1, source_target_pairs={{0,32},{32,64},{64,96},{96,128},{128,160},{160,192},{192,224},{224... | collective-permute-start | bytes 776 | tf_op jit(solution)/shard_map/while/body/eval_jaxpr/ppermute | solution.py:18
  222.9 8.9 %collective-permute-start = (bf16[64,2,256]{2,0,1:T(8,128)(2,1)S(1)}, bf16[64,2,256]{2,0,1:T(8,128)(2,1)S(1)}, u32[]{:S(2)}, u32[]{:S(2)}) collective-permute-start(bf16[64,2,256]{2,0,1:T(8,128)(2,1)S(1)} %get-tuple-element.175), channel_id=1, source_target_pairs={{0,32},{32,64},{64,96},{96,128},{128,160},{160,192},{192,224},{224... | collective-permute-start | bytes 196616 | tf_op jit(solution)/shard_map/while/body/eval_jaxpr/ppermute | solution.py:18
  234.3 8.2 %collective-permute-start.1 = (s32[64]{0:T(128)S(1)}, s32[64]{0:T(128)S(1)}, u32[]{:S(2)}, u32[]{:S(2)}) collective-permute-start(s32[64]{0:T(128)S(1)} %get-tuple-element.176), channel_id=1, source_target_pairs={{0,32},{32,64},{64,96},{96,128},{128,160},{160,192},{192,224},{224... | collective-permute-start | bytes 776 | tf_op jit(solution)/shard_map/while/body/eval_jaxpr/ppermute | solution.py:18
  236.3 8.9 %collective-permute-start = (bf16[64,2,256]{2,0,1:T(8,128)(2,1)S(1)}, bf16[64,2,256]{2,0,1:T(8,128)(2,1)S(1)}, u32[]{:S(2)}, u32[]{:S(2)}) collective-permute-start(bf16[64,2,256]{2,0,1:T(8,128)(2,1)S(1)} %get-tuple-element.175), channel_id=1, source_target_pairs={{0,32},{32,64},{64,96},{96,128},{128,160},{160,192},{192,224},{224... | collective-permute-start | bytes 196616 | tf_op jit(solution)/shard_map/while/body/eval_jaxpr/ppermute | solution.py:18
  649.7 25.3 %all-to-all-start.3 = ((bf16[8,16,2,1440]{3,2,0,1:T(2,128)(2,1)}), bf16[8,16,2,1440]{3,2,0,1:T(2,128)(2,1)S(1)}, u32[]{:S(2)}, u32[]{:S(2)}) async-start(bf16[8,16,2,1440]{3,2,0,1:T(2,128)(2,1)} %copy.72), calls=%async_computation.3 | async-start | bytes 1572864 | tf_op jit(solution)/shard_map/all_to_all | solution.py:128
  (8 other events, 500.7 us)
Sparse Core Ops, SparseCore 0:
  10.5 115.4 all-gather.1
where the time goes:
time: 690 us; the launch traced here: 689 us
  blocking collectives  350 us (51%)
  waiting for transfers between devices  151 us (22%)
  starting transfers between devices  65.6 us (10%)
  matrix products  48.6 us (7%)
  local copies, waits for them, and re-layouts  44.8 us (6%)
  between operations  13.7 us (2%)
  other arithmetic  13.4 us (2%)
    all_to_all x1, blocking collectives, body(): lax.all_to_all(copies, 'exp', split_axis=0, concat_axis=0, tiled=True)  183 us
    all_to_all x1, blocking collectives, body(): lax.all_to_all(jnp.dot(active, w_down, preferred_element_type=jnp.float32...  150 us
    ppermute x30, waiting for transfers between devices, passed_along(): lax.ppermute(value, axis, [(i, (i + by) % length) for i in range(length)])  129 us
    ppermute x30, starting transfers between devices, passed_along(): lax.ppermute(value, axis, [(i, (i + by) % length) for i in range(length)])  61.7 us
    dot_general x16, matrix products, attend_block(): jnp.einsum('gjrs,sgd->gjrd', weights, values.astype(jnp.float32), precisi...  22.6 us
    all_to_all x1, waiting for transfers between devices, body(): lax.all_to_all(result, 'ctx', split_axis=1, concat_axis=1, tiled=True)  21.3 us
    all_to_all x1, blocking collectives, body(): lax.all_to_all(outgoing, 'ctx', split_axis=1, concat_axis=1, tiled=True)  16.6 us
  transfers between devices with their start and end apart: 32, of which 31 were waited for; matrix products, arithmetic and copies ran while one was open for 8% of the time, Pallas kernels for 0%

commit v1 on v0

--- a/solution.py
+++ b/solution.py
@@ -125,7 +125,10 @@
     count = back.shape[1]
     summed = jnp.sum(back.reshape(per_row, SLICES, count, cap, D).astype(jnp.float32), axis=1)
     result = summed.astype(jnp.bfloat16)
-    returned = lax.all_to_all(result, "ctx", split_axis=1, concat_axis=1, tiled=True)
+    returned = jnp.concatenate(
+        lax.all_to_all(jnp.stack(jnp.split(result, lax.axis_size("ctx"), axis=1)), "ctx", 0, 0),
+        axis=1,
+    )
     picked = returned.reshape(n_slots, D)[slot].astype(jnp.float32).reshape(rows, TOP, D)
     final = mixed + jnp.sum(route_weights[0][:, :, None] * picked, axis=1)
     return final.astype(jnp.bfloat16)[None]

time: 690 us -> 699 us (1.013)
  local copies, waits for them, and re-layouts: 44.8 us -> 53.5 us
    unnamed x20 -> x35, local copies, waits for them, and re-layouts: 3.25 us -> 13 us
  transfers between devices with their start and end apart: 32 -> 32, of which waited for: 31 -> 31; matrix products, arithmetic and copies ran while one was open for 8% -> 7% of each run, Pallas kernels for 0% -> 0%
where the time goes in v1:
time: 699 us; the launch traced here: 698 us
  blocking collectives  350 us (50%)
  waiting for transfers between devices  151 us (22%)
  starting transfers between devices  65.8 us (9%)
  local copies, waits for them, and re-layouts  53.5 us (8%)
  matrix products  48.6 us (7%)
  between operations  13.7 us (2%)
  other arithmetic  13.4 us (2%)
    all_to_all x1, blocking collectives, body(): lax.all_to_all(copies, 'exp', split_axis=0, concat_axis=0, tiled=True)  183 us
    all_to_all x1, blocking collectives, body(): lax.all_to_all(jnp.dot(active, w_down, preferred_element_type=jnp.float32...  150 us
    ppermute x30, waiting for transfers between devices, passed_along(): lax.ppermute(value, axis, [(i, (i + by) % length) for i in range(length)])  129 us
    ppermute x30, starting transfers between devices, passed_along(): lax.ppermute(value, axis, [(i, (i + by) % length) for i in range(length)])  61.7 us
    dot_general x16, matrix products, attend_block(): jnp.einsum('gjrs,sgd->gjrd', weights, values.astype(jnp.float32), precisi...  22.6 us
    all_to_all x1, waiting for transfers between devices, body(): lax.all_to_all(jnp.stack(jnp.split(result, lax.axis_size('ctx'), axis=1))...  21.3 us
    all_to_all x1, blocking collectives, body(): lax.all_to_all(outgoing, 'ctx', split_axis=1, concat_axis=1, tiled=True)  16.6 us
  transfers between devices with their start and end apart: 32, of which 31 were waited for; matrix products, arithmetic and copies ran while one was open for 7% of the time, Pallas kernels for 0%

profile of v1, /device:TPU:1, one launch (start us, length us, event | category | flops | bytes accessed | tf_op | source)
XLA Modules:
  0.0 697.6 jit_solution(8061797299389640998)
XLA Ops:
  17.1 230.6 %while.18 = (s32[]{:T(128)}, bf16[64,2,256]{2,0,1:T(8,128)(2,1)S(1)}, s32[64]{0:T(128)S(1)}, f32[4,8,64]{2,1,0:T(8,128)S(1)}, f32[4,8,64]{2,1,0:T(8,128)S(1)}, /...) while((s32[]{:T(128)}, ...), condition=%wide.region_5.6_spmd, body=%wide.region_2.5_spmd.sunk | while | flops 118759424 | bytes 3754157 | solution.py:77
  17.1 4.4 collective-permute-start.1
  21.5 3.5 collective-permute-start
  36.8 4.8 collective-permute-done.1
  41.6 4.9 collective-permute-done
  53.0 4.8 collective-permute-done.1
  67.7 4.4 collective-permute-done.1
  81.1 6.7 collective-permute-done.1
  87.9 21.1 %collective-permute-done = bf16[64,2,256]{2,0,1:T(8,128)(2,1)S(1)} collective-permute-done((bf16[64,2,256]{2,0,1:T(8,128)(2,1)S(1)}, bf16[64,2,256]{2,0,1:T(8,128)(2,1)S(1)}, u32[]{:S(2)}, u32[]{:S(2)}) %collective-permute-start) | collective-permute-done | bytes 65568 | tf_op jit(solution)/shard_map/while/body/eval_jaxpr/ppermute | solution.py:18
  115.4 4.8 collective-permute-done.1
  120.2 4.0 collective-permute-done
  130.7 4.4 collective-permute-done.1
  144.1 4.4 collective-permute-done.1
  157.5 4.4 collective-permute-done.1
  170.8 4.4 collective-permute-done.1
  184.2 4.7 collective-permute-done.1
  197.6 4.4 collective-permute-done.1
  211.0 4.4 collective-permute-done.1
  224.8 4.4 collective-permute-done.1
  238.2 4.4 collective-permute-done.1
  252.9 4.1 multiply_reduce_fusion.1
  260.2 16.6 %all_to_all.20 = bf16[8,16,2,1440]{3,2,0,1:T(2,128)(2,1)S(1)} all-to-all(bf16[8,16,2,1440]{3,2,0,1:T(2,128)(2,1)S(1)} %copy.79), channel_id=1, replica_groups=mesh['ctx'=16,'exp'=32] {'ctx'}, dimensions={1} | all-to-all | bytes 1474560 | tf_op jit(solution)/shard_map/all_to_all | solution.py:109
  280.1 183.5 %all_to_all.21 = bf16[32,16,2,1440]{3,2,1,0:T(2,128)(2,1)} all-to-all(bf16[32,16,2,1440]{3,2,1,0:T(2,128)(2,1)S(1)} %bitcast.164), channel_id=1, replica_groups=mesh['ctx'=16,'exp'=32] {'exp'}, dimensions={0} | all-to-all | bytes 5898240 | tf_op jit(solution)/shard_map/all_to_all | solution.py:111
  463.6 7.6 %reshape.250 = bf16[1024,1440]{1,0:T(8,128)(2,1)} reshape(bf16[32,16,2,1440]{3,2,1,0:T(2,128)(2,1)} %all_to_all.21) | data formatting | bytes 5898240 | tf_op jit(solution)/shard_map/reshape | solution.py:112
  471.2 4.4 fusion.53
  475.6 7.4 %convolution_convert_fusion = bf16[1024,1440]{0,1:T(8,128)(2,1)} fusion(bf16[360,1440]{1,0:T(8,128)(2,1)S(1)} %copy-done, f32[1024,360]{0,1:T(8,128)} %fusion.53, bf16[1024,1440]{1,0:T(8,128)(2,1)} %reshape.250, bf16[1440,360]{1,0:T(8,128)(2,1)} %param.24), kind=kOutput, calls=%fused_computation.19 | convolution fusion | flops 2127790080 | bytes 9446400 | tf_op jit(solution)/shard_map/dot_general | solution.py:117
  482.9 4.6 copy.81
  487.5 7.3 %reshape.251 = bf16[32,16,2,1440]{3,2,1,0:T(2,128)(2,1)} reshape(bf16[1024,1440]{1,0:T(8,128)(2,1)} %copy.81) | data formatting | bytes 5898240 | tf_op jit(solution)/shard_map/reshape | solution.py:119
  494.9 149.7 %all_to_all.22 = bf16[32,16,2,1440]{3,2,1,0:T(2,128)(2,1)S(1)} all-to-all(bf16[32,16,2,1440]{3,2,1,0:T(2,128)(2,1)} %reshape.251), channel_id=1, replica_groups=mesh['ctx'=16,'exp'=32] {'exp'}, dimensions={0} | all-to-all | bytes 5898240 | tf_op jit(solution)/shard_map/all_to_all | solution.py:116
  644.5 3.5 bitcast_reduce_fusion
  658.4 4.1 all-to-all-start.3
  662.7 21.3 %all-to-all-done.3 = bf16[16,8,1,2,1440]{4,3,1,2,0:T(2,128)(2,1)S(1)} async-done(((bf16[16,8,1,2,1440]{4,3,1,2,0:T(2,128)(2,1)}), bf16[16,8,1,2,1440]{4,3,1,2,0:T(2,128)(2,1)S(1)}, u32[]{:S(2)}, u32[]{:S(2)}) %all-to-all-start.3) | async-done | bytes 737312 | tf_op jit(solution)/shard_map/all_to_all | solution.py:129
  (309 shorter events, 165.4 us)
Async XLA Ops:
  6.5 246.3 %all-gather.2.cloned.1.call-start = ((), (), s32[]{:S(2)}) async-start(), calls=%async_computation.4 | async-start | bytes 6488064 | tf_op jit(solution)/shard_map/all_gather | solution.py:83
  17.1 10.5 %collective-permute-start.1 = (s32[64]{0:T(128)S(1)}, s32[64]{0:T(128)S(1)}, u32[]{:S(2)}, u32[]{:S(2)}) collective-permute-start(s32[64]{0:T(128)S(1)} %get-tuple-element.170), channel_id=1, source_target_pairs={{0,32},{32,64},{64,96},{96,128},{128,160},{160,192},{192,224},{224... | collective-permute-start | bytes 776 | tf_op jit(solution)/shard_map/while/body/eval_jaxpr/ppermute | solution.py:18
  21.5 8.9 %collective-permute-start = (bf16[64,2,256]{2,0,1:T(8,128)(2,1)S(1)}, bf16[64,2,256]{2,0,1:T(8,128)(2,1)S(1)}, u32[]{:S(2)}, u32[]{:S(2)}) collective-permute-start(bf16[64,2,256]{2,0,1:T(8,128)(2,1)S(1)} %get-tuple-element.169), channel_id=1, source_target_pairs={{0,32},{32,64},{64,96},{96,128},{128,160},{160,192},{192,224},{224... | collective-permute-start | bytes 196616 | tf_op jit(solution)/shard_map/while/body/eval_jaxpr/ppermute | solution.py:18
  32.9 8.6 %collective-permute-start.1 = (s32[64]{0:T(128)S(1)}, s32[64]{0:T(128)S(1)}, u32[]{:S(2)}, u32[]{:S(2)}) collective-permute-start(s32[64]{0:T(128)S(1)} %get-tuple-element.170), channel_id=1, source_target_pairs={{0,32},{32,64},{64,96},{96,128},{128,160},{160,192},{192,224},{224... | collective-permute-start | bytes 776 | tf_op jit(solution)/shard_map/while/body/eval_jaxpr/ppermute | solution.py:18
  34.8 11.7 %collective-permute-start = (bf16[64,2,256]{2,0,1:T(8,128)(2,1)S(1)}, bf16[64,2,256]{2,0,1:T(8,128)(2,1)S(1)}, u32[]{:S(2)}, u32[]{:S(2)}) collective-permute-start(bf16[64,2,256]{2,0,1:T(8,128)(2,1)S(1)} %get-tuple-element.169), channel_id=1, source_target_pairs={{0,32},{32,64},{64,96},{96,128},{128,160},{160,192},{192,224},{224... | collective-permute-start | bytes 196616 | tf_op jit(solution)/shard_map/while/body/eval_jaxpr/ppermute | solution.py:18
  49.1 8.6 %collective-permute-start.1 = (s32[64]{0:T(128)S(1)}, s32[64]{0:T(128)S(1)}, u32[]{:S(2)}, u32[]{:S(2)}) collective-permute-start(s32[64]{0:T(128)S(1)} %get-tuple-element.170), channel_id=1, source_target_pairs={{0,32},{32,64},{64,96},{96,128},{128,160},{160,192},{192,224},{224... | collective-permute-start | bytes 776 | tf_op jit(solution)/shard_map/while/body/eval_jaxpr/ppermute | solution.py:18
  51.0 10.3 %collective-permute-start = (bf16[64,2,256]{2,0,1:T(8,128)(2,1)S(1)}, bf16[64,2,256]{2,0,1:T(8,128)(2,1)S(1)}, u32[]{:S(2)}, u32[]{:S(2)}) collective-permute-start(bf16[64,2,256]{2,0,1:T(8,128)(2,1)S(1)} %get-tuple-element.169), channel_id=1, source_target_pairs={{0,32},{32,64},{64,96},{96,128},{128,160},{160,192},{192,224},{224... | collective-permute-start | bytes 196616 | tf_op jit(solution)/shard_map/while/body/eval_jaxpr/ppermute | solution.py:18
  63.8 8.2 %collective-permute-start.1 = (s32[64]{0:T(128)S(1)}, s32[64]{0:T(128)S(1)}, u32[]{:S(2)}, u32[]{:S(2)}) collective-permute-start(s32[64]{0:T(128)S(1)} %get-tuple-element.170), channel_id=1, source_target_pairs={{0,32},{32,64},{64,96},{96,128},{128,160},{160,192},{192,224},{224... | collective-permute-start | bytes 776 | tf_op jit(solution)/shard_map/while/body/eval_jaxpr/ppermute | solution.py:18
  65.8 8.9 %collective-permute-start = (bf16[64,2,256]{2,0,1:T(8,128)(2,1)S(1)}, bf16[64,2,256]{2,0,1:T(8,128)(2,1)S(1)}, u32[]{:S(2)}, u32[]{:S(2)}) collective-permute-start(bf16[64,2,256]{2,0,1:T(8,128)(2,1)S(1)} %get-tuple-element.169), channel_id=1, source_target_pairs={{0,32},{32,64},{64,96},{96,128},{128,160},{160,192},{192,224},{224... | collective-permute-start | bytes 196616 | tf_op jit(solution)/shard_map/while/body/eval_jaxpr/ppermute | solution.py:18
  77.2 10.6 %collective-permute-start.1 = (s32[64]{0:T(128)S(1)}, s32[64]{0:T(128)S(1)}, u32[]{:S(2)}, u32[]{:S(2)}) collective-permute-start(s32[64]{0:T(128)S(1)} %get-tuple-element.170), channel_id=1, source_target_pairs={{0,32},{32,64},{64,96},{96,128},{128,160},{160,192},{192,224},{224... | collective-permute-start | bytes 776 | tf_op jit(solution)/shard_map/while/body/eval_jaxpr/ppermute | solution.py:18
  79.2 29.8 %collective-permute-start = (bf16[64,2,256]{2,0,1:T(8,128)(2,1)S(1)}, bf16[64,2,256]{2,0,1:T(8,128)(2,1)S(1)}, u32[]{:S(2)}, u32[]{:S(2)}) collective-permute-start(bf16[64,2,256]{2,0,1:T(8,128)(2,1)S(1)} %get-tuple-element.169), channel_id=1, source_target_pairs={{0,32},{32,64},{64,96},{96,128},{128,160},{160,192},{192,224},{224... | collective-permute-start | bytes 196616 | tf_op jit(solution)/shard_map/while/body/eval_jaxpr/ppermute | solution.py:18
  111.5 8.6 %collective-permute-start.1 = (s32[64]{0:T(128)S(1)}, s32[64]{0:T(128)S(1)}, u32[]{:S(2)}, u32[]{:S(2)}) collective-permute-start(s32[64]{0:T(128)S(1)} %get-tuple-element.170), channel_id=1, source_target_pairs={{0,32},{32,64},{64,96},{96,128},{128,160},{160,192},{192,224},{224... | collective-permute-start | bytes 776 | tf_op jit(solution)/shard_map/while/body/eval_jaxpr/ppermute | solution.py:18
  113.5 10.8 %collective-permute-start = (bf16[64,2,256]{2,0,1:T(8,128)(2,1)S(1)}, bf16[64,2,256]{2,0,1:T(8,128)(2,1)S(1)}, u32[]{:S(2)}, u32[]{:S(2)}) collective-permute-start(bf16[64,2,256]{2,0,1:T(8,128)(2,1)S(1)} %get-tuple-element.169), channel_id=1, source_target_pairs={{0,32},{32,64},{64,96},{96,128},{128,160},{160,192},{192,224},{224... | collective-permute-start | bytes 196616 | tf_op jit(solution)/shard_map/while/body/eval_jaxpr/ppermute | solution.py:18
  126.8 8.2 %collective-permute-start.1 = (s32[64]{0:T(128)S(1)}, s32[64]{0:T(128)S(1)}, u32[]{:S(2)}, u32[]{:S(2)}) collective-permute-start(s32[64]{0:T(128)S(1)} %get-tuple-element.170), channel_id=1, source_target_pairs={{0,32},{32,64},{64,96},{96,128},{128,160},{160,192},{192,224},{224... | collective-permute-start | bytes 776 | tf_op jit(solution)/shard_map/while/body/eval_jaxpr/ppermute | solution.py:18
  128.7 8.9 %collective-permute-start = (bf16[64,2,256]{2,0,1:T(8,128)(2,1)S(1)}, bf16[64,2,256]{2,0,1:T(8,128)(2,1)S(1)}, u32[]{:S(2)}, u32[]{:S(2)}) collective-permute-start(bf16[64,2,256]{2,0,1:T(8,128)(2,1)S(1)} %get-tuple-element.169), channel_id=1, source_target_pairs={{0,32},{32,64},{64,96},{96,128},{128,160},{160,192},{192,224},{224... | collective-permute-start | bytes 196616 | tf_op jit(solution)/shard_map/while/body/eval_jaxpr/ppermute | solution.py:18
  140.2 8.2 %collective-permute-start.1 = (s32[64]{0:T(128)S(1)}, s32[64]{0:T(128)S(1)}, u32[]{:S(2)}, u32[]{:S(2)}) collective-permute-start(s32[64]{0:T(128)S(1)} %get-tuple-element.170), channel_id=1, source_target_pairs={{0,32},{32,64},{64,96},{96,128},{128,160},{160,192},{192,224},{224... | collective-permute-start | bytes 776 | tf_op jit(solution)/shard_map/while/body/eval_jaxpr/ppermute | solution.py:18
  142.1 8.9 %collective-permute-start = (bf16[64,2,256]{2,0,1:T(8,128)(2,1)S(1)}, bf16[64,2,256]{2,0,1:T(8,128)(2,1)S(1)}, u32[]{:S(2)}, u32[]{:S(2)}) collective-permute-start(bf16[64,2,256]{2,0,1:T(8,128)(2,1)S(1)} %get-tuple-element.169), channel_id=1, source_target_pairs={{0,32},{32,64},{64,96},{96,128},{128,160},{160,192},{192,224},{224... | collective-permute-start | bytes 196616 | tf_op jit(solution)/shard_map/while/body/eval_jaxpr/ppermute | solution.py:18
  153.6 8.2 %collective-permute-start.1 = (s32[64]{0:T(128)S(1)}, s32[64]{0:T(128)S(1)}, u32[]{:S(2)}, u32[]{:S(2)}) collective-permute-start(s32[64]{0:T(128)S(1)} %get-tuple-element.170), channel_id=1, source_target_pairs={{0,32},{32,64},{64,96},{96,128},{128,160},{160,192},{192,224},{224... | collective-permute-start | bytes 776 | tf_op jit(solution)/shard_map/while/body/eval_jaxpr/ppermute | solution.py:18
  155.5 8.9 %collective-permute-start = (bf16[64,2,256]{2,0,1:T(8,128)(2,1)S(1)}, bf16[64,2,256]{2,0,1:T(8,128)(2,1)S(1)}, u32[]{:S(2)}, u32[]{:S(2)}) collective-permute-start(bf16[64,2,256]{2,0,1:T(8,128)(2,1)S(1)} %get-tuple-element.169), channel_id=1, source_target_pairs={{0,32},{32,64},{64,96},{96,128},{128,160},{160,192},{192,224},{224... | collective-permute-start | bytes 196616 | tf_op jit(solution)/shard_map/while/body/eval_jaxpr/ppermute | solution.py:18
  167.0 8.2 %collective-permute-start.1 = (s32[64]{0:T(128)S(1)}, s32[64]{0:T(128)S(1)}, u32[]{:S(2)}, u32[]{:S(2)}) collective-permute-start(s32[64]{0:T(128)S(1)} %get-tuple-element.170), channel_id=1, source_target_pairs={{0,32},{32,64},{64,96},{96,128},{128,160},{160,192},{192,224},{224... | collective-permute-start | bytes 776 | tf_op jit(solution)/shard_map/while/body/eval_jaxpr/ppermute | solution.py:18
  168.9 8.9 %collective-permute-start = (bf16[64,2,256]{2,0,1:T(8,128)(2,1)S(1)}, bf16[64,2,256]{2,0,1:T(8,128)(2,1)S(1)}, u32[]{:S(2)}, u32[]{:S(2)}) collective-permute-start(bf16[64,2,256]{2,0,1:T(8,128)(2,1)S(1)} %get-tuple-element.169), channel_id=1, source_target_pairs={{0,32},{32,64},{64,96},{96,128},{128,160},{160,192},{192,224},{224... | collective-permute-start | bytes 196616 | tf_op jit(solution)/shard_map/while/body/eval_jaxpr/ppermute | solution.py:18
  180.4 8.5 %collective-permute-start.1 = (s32[64]{0:T(128)S(1)}, s32[64]{0:T(128)S(1)}, u32[]{:S(2)}, u32[]{:S(2)}) collective-permute-start(s32[64]{0:T(128)S(1)} %get-tuple-element.170), channel_id=1, source_target_pairs={{0,32},{32,64},{64,96},{96,128},{128,160},{160,192},{192,224},{224... | collective-permute-start | bytes 776 | tf_op jit(solution)/shard_map/while/body/eval_jaxpr/ppermute | solution.py:18
  182.3 8.9 %collective-permute-start = (bf16[64,2,256]{2,0,1:T(8,128)(2,1)S(1)}, bf16[64,2,256]{2,0,1:T(8,128)(2,1)S(1)}, u32[]{:S(2)}, u32[]{:S(2)}) collective-permute-start(bf16[64,2,256]{2,0,1:T(8,128)(2,1)S(1)} %get-tuple-element.169), channel_id=1, source_target_pairs={{0,32},{32,64},{64,96},{96,128},{128,160},{160,192},{192,224},{224... | collective-permute-start | bytes 196616 | tf_op jit(solution)/shard_map/while/body/eval_jaxpr/ppermute | solution.py:18
  193.8 8.2 %collective-permute-start.1 = (s32[64]{0:T(128)S(1)}, s32[64]{0:T(128)S(1)}, u32[]{:S(2)}, u32[]{:S(2)}) collective-permute-start(s32[64]{0:T(128)S(1)} %get-tuple-element.170), channel_id=1, source_target_pairs={{0,32},{32,64},{64,96},{96,128},{128,160},{160,192},{192,224},{224... | collective-permute-start | bytes 776 | tf_op jit(solution)/shard_map/while/body/eval_jaxpr/ppermute | solution.py:18
  195.7 8.9 %collective-permute-start = (bf16[64,2,256]{2,0,1:T(8,128)(2,1)S(1)}, bf16[64,2,256]{2,0,1:T(8,128)(2,1)S(1)}, u32[]{:S(2)}, u32[]{:S(2)}) collective-permute-start(bf16[64,2,256]{2,0,1:T(8,128)(2,1)S(1)} %get-tuple-element.169), channel_id=1, source_target_pairs={{0,32},{32,64},{64,96},{96,128},{128,160},{160,192},{192,224},{224... | collective-permute-start | bytes 196616 | tf_op jit(solution)/shard_map/while/body/eval_jaxpr/ppermute | solution.py:18
  207.2 8.2 %collective-permute-start.1 = (s32[64]{0:T(128)S(1)}, s32[64]{0:T(128)S(1)}, u32[]{:S(2)}, u32[]{:S(2)}) collective-permute-start(s32[64]{0:T(128)S(1)} %get-tuple-element.170), channel_id=1, source_target_pairs={{0,32},{32,64},{64,96},{96,128},{128,160},{160,192},{192,224},{224... | collective-permute-start | bytes 776 | tf_op jit(solution)/shard_map/while/body/eval_jaxpr/ppermute | solution.py:18
  209.1 9.3 %collective-permute-start = (bf16[64,2,256]{2,0,1:T(8,128)(2,1)S(1)}, bf16[64,2,256]{2,0,1:T(8,128)(2,1)S(1)}, u32[]{:S(2)}, u32[]{:S(2)}) collective-permute-start(bf16[64,2,256]{2,0,1:T(8,128)(2,1)S(1)} %get-tuple-element.169), channel_id=1, source_target_pairs={{0,32},{32,64},{64,96},{96,128},{128,160},{160,192},{192,224},{224... | collective-permute-start | bytes 196616 | tf_op jit(solution)/shard_map/while/body/eval_jaxpr/ppermute | solution.py:18
  220.9 8.2 %collective-permute-start.1 = (s32[64]{0:T(128)S(1)}, s32[64]{0:T(128)S(1)}, u32[]{:S(2)}, u32[]{:S(2)}) collective-permute-start(s32[64]{0:T(128)S(1)} %get-tuple-element.170), channel_id=1, source_target_pairs={{0,32},{32,64},{64,96},{96,128},{128,160},{160,192},{192,224},{224... | collective-permute-start | bytes 776 | tf_op jit(solution)/shard_map/while/body/eval_jaxpr/ppermute | solution.py:18
  222.9 8.9 %collective-permute-start = (bf16[64,2,256]{2,0,1:T(8,128)(2,1)S(1)}, bf16[64,2,256]{2,0,1:T(8,128)(2,1)S(1)}, u32[]{:S(2)}, u32[]{:S(2)}) collective-permute-start(bf16[64,2,256]{2,0,1:T(8,128)(2,1)S(1)} %get-tuple-element.169), channel_id=1, source_target_pairs={{0,32},{32,64},{64,96},{96,128},{128,160},{160,192},{192,224},{224... | collective-permute-start | bytes 196616 | tf_op jit(solution)/shard_map/while/body/eval_jaxpr/ppermute | solution.py:18
  234.3 8.2 %collective-permute-start.1 = (s32[64]{0:T(128)S(1)}, s32[64]{0:T(128)S(1)}, u32[]{:S(2)}, u32[]{:S(2)}) collective-permute-start(s32[64]{0:T(128)S(1)} %get-tuple-element.170), channel_id=1, source_target_pairs={{0,32},{32,64},{64,96},{96,128},{128,160},{160,192},{192,224},{224... | collective-permute-start | bytes 776 | tf_op jit(solution)/shard_map/while/body/eval_jaxpr/ppermute | solution.py:18
  236.3 8.9 %collective-permute-start = (bf16[64,2,256]{2,0,1:T(8,128)(2,1)S(1)}, bf16[64,2,256]{2,0,1:T(8,128)(2,1)S(1)}, u32[]{:S(2)}, u32[]{:S(2)}) collective-permute-start(bf16[64,2,256]{2,0,1:T(8,128)(2,1)S(1)} %get-tuple-element.169), channel_id=1, source_target_pairs={{0,32},{32,64},{64,96},{96,128},{128,160},{160,192},{192,224},{224... | collective-permute-start | bytes 196616 | tf_op jit(solution)/shard_map/while/body/eval_jaxpr/ppermute | solution.py:18
  658.4 25.5 %all-to-all-start.3 = ((bf16[16,8,1,2,1440]{4,3,1,2,0:T(2,128)(2,1)}), bf16[16,8,1,2,1440]{4,3,1,2,0:T(2,128)(2,1)S(1)}, u32[]{:S(2)}, u32[]{:S(2)}) async-start(bf16[16,8,1,2,1440]{4,3,1,2,0:T(2,128)(2,1)} %fusion.23), calls=%async_computation.3 | async-start | bytes 1572864 | tf_op jit(solution)/shard_map/all_to_all | solution.py:129
  (8 other events, 508.4 us)
Sparse Core Ops, SparseCore 0:
  10.5 115.4 all-gather.1
